TPU v7x, 32 devices: a whole 2x2x4 slice. The times are simulated.
32 devices in a mesh: gx: 4 (over y, x), gy: 8 (over z, core).
Axes of the slice: x: 2, y: 2, z: 4, core: 2. Of those that a mesh axis runs over, the one named last changes fastest.
Arguments:
- stream: bfloat16 [768, 4096], P('gy', 'gx'), may hold values from -40 to 40
- qkv_weight: bfloat16 [4096, 12288], P('gx', 'gy'), may hold values from -0.1875 to 0.1875
- up_weight: bfloat16 [4096, 16384], P('gx', 'gy'), may hold values from -0.09375 to 0.09375
- out_weight: bfloat16 [4096, 4096], P('gy', 'gx'), may hold values from -0.09375 to 0.09375
- down_weight: bfloat16 [16384, 4096], P('gy', 'gx'), may hold values from -0.046875 to 0.046875
- cache_keys: bfloat16 [896, 4096], P('gx', 'gy'), may hold values from -400 to 400
- cache_values: bfloat16 [896, 4096], P('gx', 'gy'), may hold values from -12 to 12
- request_prefix: int32 [6], replicated, may hold values from 0 to 1
- request_lengths: int32 [6], replicated, may hold values from 1 to 192, 768 in all
- owner_list: int32 [4], replicated, may hold values from 0 to 3, each once
Outputs:
- layer_out: float32 [768, 4096], P('gy', 'gx')
Inputs may be any that keep to these rules, and one draw needn't show every extreme that they name: `request_lengths`: they sum to 768, and the largest is exactly 192. `owner_list`: each of 0 to 3 appears once.
All inputs are finite; a program needn't handle non-finite values.
Results may differ from a plain program's by a relative error of at most 0.0084.
Values may be sent and summed in bfloat16 or wider, within the bound.
No kernel may reach another device: no remote copies, remote signals or barrier semaphores. Data moves between devices by JAX's collectives and lax.ppermute only.
A program may use at most 128 MiB of HBM per device.

v0:
```python
import jax
import jax.numpy as jnp
from jax import lax
from jax.sharding import PartitionSpec as P

HD = 128
ROT = 32
epsilon = 1e-05
rotary_base = 10000.0
masked_score = -1e30


def token_layout(request_lengths, token_count):
    ending = jnp.cumsum(request_lengths)
    starting = ending - request_lengths
    token_ids = jnp.arange(token_count, dtype=jnp.int32)
    segment = jnp.sum((token_ids[:, None] >= ending[None, :]).astype(jnp.int32), axis=1)
    member = segment[:, None] == jnp.arange(request_lengths.shape[0], dtype=jnp.int32)[None, :]
    first_token = jnp.sum(jnp.where(member, starting[None, :], 0), axis=1)
    return (token_ids, segment, token_ids - first_token, member)


def rotate(vectors, angle_pos):
    halfway = ROT // 2
    frequency = rotary_base ** (-2.0 * jnp.arange(halfway, dtype=jnp.float32) / ROT)
    angles = angle_pos[:, None] * frequency[None, :]
    cosine = jnp.cos(angles)[:, None, :]
    sine_part = jnp.sin(angles)[:, None, :]
    leading = vectors[..., :halfway]
    trailing = vectors[..., halfway:ROT]
    return jnp.concatenate(
        [
            leading * cosine - trailing * sine_part,
            trailing * cosine + leading * sine_part,
            vectors[..., ROT:],
        ],
        axis=-1,
    )


def split_heads(head_block, angle_pos, head_count):
    rows_here = head_block.shape[0]
    head_parts = head_block.reshape(rows_here, head_count, 3, HD)
    queries = rotate(head_parts[:, :, 0], angle_pos).astype(jnp.bfloat16)
    keys_new = rotate(head_parts[:, :, 1], angle_pos).astype(jnp.bfloat16)
    values_new = head_parts[:, :, 2].astype(jnp.bfloat16)
    return (queries, keys_new, values_new)


def shards(
    stream,
    qkv_weight,
    up_weight,
    out_weight,
    down_weight,
    cache_keys,
    cache_values,
    request_prefix,
    request_lengths,
    owner_list,
):
    groups = lax.axis_size("gx")
    group_index = lax.axis_index("gx")
    local_rows = stream.shape[0]
    feature_count = stream.shape[1] * groups
    token_count = local_rows * lax.axis_size("gy")
    share_rows = token_count // groups
    head_cols = qkv_weight.shape[1]
    head_count = head_cols // (3 * HD)
    block_len = cache_keys.shape[0]
    prefix_len = block_len * groups // 2
    score_scale = HD ** (-0.5)
    values32 = stream.astype(jnp.float32)
    moments = lax.psum((jnp.sum(values32, axis=1), jnp.sum(values32 * values32, axis=1)), "gx")
    average = (moments[0] / feature_count)[:, None]
    square = (moments[1] / feature_count)[:, None]
    normed = ((values32 - average) * lax.rsqrt(square - average * average + epsilon)).astype(
        jnp.bfloat16
    )
    row_piece = lax.all_gather(normed, "gy", axis=0, tiled=True)
    partial_sums = jnp.concatenate(
        [
            jnp.dot(row_piece, qkv_weight, preferred_element_type=jnp.float32),
            jnp.dot(row_piece, up_weight, preferred_element_type=jnp.float32),
        ],
        axis=1,
    )
    token_ids, segment, offsets, member = token_layout(request_lengths, token_count)
    angle_pos = (offsets + prefix_len).astype(jnp.float32)
    first_row = group_index * share_rows
    summed = lax.psum_scatter(partial_sums, "gx", scatter_dimension=0, tiled=True)
    up_own = summed[:, head_cols:]
    own_angles = lax.dynamic_slice_in_dim(angle_pos, first_row, share_rows)
    own_query, own_keys, own_values = split_heads(summed[:, :head_cols], own_angles, head_count)
    queries, keys_new, values_new = (
        lax.all_gather(own_query, "gx", axis=0, tiled=True),
        lax.all_gather(own_keys, "gx", axis=0, tiled=True),
        lax.all_gather(own_values, "gx", axis=0, tiled=True),
    )
    hidden_own = jax.nn.gelu(up_own, approximate=False).astype(jnp.bfloat16)
    mine_query = lax.dynamic_slice_in_dim(queries, first_row, share_rows)
    mine_ids = lax.dynamic_slice_in_dim(token_ids, first_row, share_rows)
    mine_segment = lax.dynamic_slice_in_dim(segment, first_row, share_rows)
    visible = (mine_segment[:, None] == segment[None, :]) & (
        token_ids[None, :] <= mine_ids[:, None]
    )
    recent = (
        jnp.einsum("qhd,khd->hqk", mine_query, keys_new, preferred_element_type=jnp.float32)
        * score_scale
    )
    recent = jnp.where(visible[None], recent, masked_score)
    recent_peak = jnp.max(recent, axis=2)
    recent_weights = jnp.exp(recent - recent_peak[..., None])
    recent_total = jnp.sum(recent_weights, axis=2)
    recent_out = jnp.einsum(
        "hqk,khd->hqd",
        recent_weights.astype(jnp.bfloat16),
        values_new,
        preferred_element_type=jnp.float32,
    )
    halfway = groups // 2
    slot_index = jnp.arange(groups, dtype=jnp.int32)
    held_prefix = jnp.sum(
        jnp.where(owner_list == group_index, (slot_index >= halfway).astype(jnp.int32), 0)
    )
    token_prefix = jnp.sum(jnp.where(member, request_prefix[None, :], 0), axis=1)
    active = (token_prefix == held_prefix)[None, :, None]
    step_len = min(512, block_len)
    key_blocks = cache_keys.reshape(block_len // step_len, step_len, head_count, HD)
    value_blocks = cache_values.reshape(block_len // step_len, step_len, head_count, HD)

    def visit(carried, blocks):
        run_peak, run_total, run_out = carried
        block_keys, block_values = blocks
        scores = (
            jnp.einsum("qhd,khd->hqk", queries, block_keys, preferred_element_type=jnp.float32)
            * score_scale
        )
        scores = jnp.where(active, scores, masked_score)
        new_peak = jnp.maximum(run_peak, jnp.max(scores, axis=2))
        fading = jnp.exp(run_peak - new_peak)
        weights = jnp.exp(scores - new_peak[..., None])
        run_total = run_total * fading + jnp.sum(weights, axis=2)
        run_out = run_out * fading[..., None] + jnp.einsum(
            "hqk,khd->hqd",
            weights.astype(jnp.bfloat16),
            block_values,
            preferred_element_type=jnp.float32,
        )
        return ((new_peak, run_total, run_out), None)

    start_carry = (
        jnp.full((head_count, token_count), masked_score, jnp.float32),
        jnp.zeros((head_count, token_count), jnp.float32),
        jnp.zeros((head_count, token_count, HD), jnp.float32),
    )
    (cache_peak, cache_total, cache_out), unused = lax.scan(
        visit, start_carry, (key_blocks, value_blocks)
    )
    global_peak = lax.pmax(cache_peak, "gx")
    fading = jnp.exp(cache_peak - global_peak)
    own_total, own_out = (
        lax.psum_scatter(
            (cache_total * fading).astype(jnp.bfloat16), "gx", scatter_dimension=1, tiled=True
        ).astype(jnp.float32),
        lax.psum_scatter(
            (cache_out * fading[..., None]).astype(jnp.bfloat16),
            "gx",
            scatter_dimension=1,
            tiled=True,
        ).astype(jnp.float32),
    )
    own_peak = lax.dynamic_slice_in_dim(global_peak, first_row, share_rows, 1)
    joint_peak = jnp.maximum(own_peak, recent_peak)
    cache_fade = jnp.exp(own_peak - joint_peak)
    recent_fade = jnp.exp(recent_peak - joint_peak)
    context = (own_out * cache_fade[..., None] + recent_out * recent_fade[..., None]) / (
        own_total * cache_fade + recent_total * recent_fade
    )[..., None]
    context = (
        jnp.transpose(context, (1, 0, 2)).reshape(share_rows, head_count * HD).astype(jnp.bfloat16)
    )
    joined = jnp.concatenate([context, hidden_own], axis=1)
    gathered = lax.all_gather(joined, "gx", axis=0, tiled=True)
    context_cols = context.shape[1]
    row_piece = gathered
    mixed_sum = lax.psum_scatter(
        (
            jnp.dot(row_piece[:, :context_cols], out_weight, preferred_element_type=jnp.float32)
            + jnp.dot(row_piece[:, context_cols:], down_weight, preferred_element_type=jnp.float32)
        ).astype(jnp.bfloat16),
        "gy",
        scatter_dimension=0,
        tiled=True,
    ).astype(jnp.float32)
    return values32 + mixed_sum


def solution(mesh):
    placed = (
        P("gy", "gx"),
        P("gx", "gy"),
        P("gx", "gy"),
        P("gy", "gx"),
        P("gy", "gx"),
        P("gx", "gy"),
        P("gx", "gy"),
        P(),
        P(),
        P(),
    )
    return jax.shard_map(
        shards, mesh=mesh, in_specs=placed, out_specs=P("gy", "gx"), check_vma=False
    )
```

profile of v0, /device:TPU:0, one launch (start us, length us, event | category | flops | bytes accessed | tf_op | source)
XLA Modules:
  0.0 387.8 jit_solution(503710004376273790)
XLA Ops:
  7.8 11.4 %all-reduce = (f32[96]{0:T(128)S(1)}, f32[96]{0:T(128)S(1)}) all-reduce(f32[96]{0:T(128)S(1)} %get-tuple-element.20, f32[96]{0:T(128)S(1)} %get-tuple-element.19), channel_id=1, replica_groups=mesh['gx'=4,'gy'=8] {'gx'}, use_global_device_ids=true, to_apply=%region_7.8 | all-reduce | flops 192 | bytes 1536 | tf_op jit(solution)/shard_map/psum | solution.py:74
  21.0 24.5 %all-gather.4.cloned.1.call-done = bf16[768,1024]{1,0:T(8,128)(2,1)} async-done(((bf16[96,1024]{1,0:T(8,128)(2,1)}), bf16[768,1024]{1,0:T(8,128)(2,1)}) %all-gather.4.cloned.1.call-update) | async-done | bytes 1572880 | tf_op jit(solution)/shard_map/all_gather | solution.py:80
  45.5 8.8 %fusion.61 = f32[768,2048]{1,0:T(8,128)} fusion(bf16[768,1024]{1,0:T(8,128)(2,1)} %all-gather.4.cloned.1.call-done, bf16[1024,2048]{1,0:T(8,128)(2,1)} %param.12), kind=kOutput, calls=%fused_computation.110 | convolution fusion | flops 3221225472 | bytes 12058624 | tf_op jit(solution)/shard_map/dot_general | solution.py:84
  54.3 4.3 %fusion.60 = f32[768,1536]{1,0:T(8,128)} fusion(bf16[768,1024]{1,0:T(8,128)(2,1)S(1)} %copy-done.8, bf16[1024,1536]{1,0:T(8,128)(2,1)S(1)} %copy-done), kind=kOutput, calls=%fused_computation.109 | convolution fusion | flops 2415919104 | bytes 9437184 | tf_op jit(solution)/shard_map/dot_general | solution.py:83
  58.6 9.1 %pad_maximum_fusion = f32[768,3584]{1,0:T(8,128)} fusion(f32[768,2048]{1,0:T(8,128)} %fusion.61, f32[768,1536]{1,0:T(8,128)} %fusion.60), kind=kLoop, calls=%fused_computation | loop fusion | flops 2752512 | bytes 22020096 | tf_op jit(solution)/shard_map/concatenate | solution.py:81
  70.9 104.4 %reduce-scatter.7.cloned.1.call-done = f32[192,3584]{1,0:T(8,128)} async-done(((f32[768,3584]{1,0:T(8,128)}), f32[192,3584]{1,0:T(8,128)}) %reduce-scatter.7.cloned.1.call-update) | async-done | bytes 2752528 | tf_op jit(solution)/shard_map/reduce_scatter | solution.py:91
  175.3 2.4 slice.55
  177.7 2.8 reshape.155
  180.5 2.6 fusion.59
  183.9 11.2 %all_gather.16 = bf16[768,4,128]{2,0,1:T(8,128)(2,1)S(1)} all-gather(bf16[192,4,128]{2,0,1:T(8,128)(2,1)S(1)} %pad_maximum_fusion.2), channel_id=1, replica_groups=mesh['gx'=4,'gy'=8] {'gx'}, dimensions={0}, use_global_device_ids=true | all-gather | bytes 983040 | tf_op jit(solution)/shard_map/all_gather | solution.py:96
  195.3 11.6 %all_gather.17 = bf16[768,4,128]{2,0,1:T(8,128)(2,1)} all-gather(bf16[192,4,128]{2,0,1:T(8,128)(2,1)S(1)} %pad_maximum_fusion.3), channel_id=1, replica_groups=mesh['gx'=4,'gy'=8] {'gx'}, dimensions={0}, use_global_device_ids=true | all-gather | bytes 983040 | tf_op jit(solution)/shard_map/all_gather | solution.py:97
  209.0 15.2 %pmax.7 = f32[4,768]{1,0:T(4,128)S(1)} all-reduce(f32[4,768]{1,0:T(4,128)S(1)} %broadcast_maximum_fusion), channel_id=1, replica_groups=mesh['gx'=4,'gy'=8] {'gx'}, use_global_device_ids=true, to_apply=%region_11.12 | all-reduce | flops 3072 | bytes 24576 | tf_op jit(solution)/shard_map/pmax | solution.py:160
  224.2 2.3 fusion.3
  227.7 4.2 %multiply_convert_fusion = bf16[4,768,128]{2,1,0:T(8,128)(2,1)} fusion(f32[4,768,224]{1,2,0:T(8,128)} %get-tuple-element.56, f32[4,768]{1,0:T(4,128)S(1)} %broadcast_maximum_fusion, pred[768]{0:T(1024)(128)(4,1)S(1)} %broadcast_compare_fusion, f32[4,768]{1,0:T(4,128)S(1)} %get-tuple-element.39, f32[4,768]{1,0:T(4,128)S(1)} %get-tuple-element.48, ...), kind=kOutput, calls=%fused_computation.31 | convolution fusion | flops 180092928 | bytes 3805952 | tf_op jit(solution)/shard_map/while/body/eval_jaxpr/hqk,khd->hqd/dot_general | solution.py:144
  231.9 3.2 fusion.5
  237.1 11.9 %all-gather = bf16[768,4,1,128]{3,0,1,2:T(8,128)(2,1)} all-gather(bf16[192,4,1,128]{3,0,1,2:T(8,128)(2,1)S(1)} %copy.63), channel_id=2, replica_groups=mesh['gx'=4,'gy'=8] {'gx'}, dimensions={0}, use_global_device_ids=true | all-gather | bytes 983040 | tf_op jit(solution)/shard_map/all_gather | solution.py:98
  249.0 2.4 fusion.6
  251.4 4.1 %fusion.10 = bf16[192,2048]{1,0:T(8,128)(2,1)} fusion(f32[192,3584]{1,0:T(8,128)S(1)} %copy-done.3), kind=kLoop, calls=%fused_computation.17 | loop fusion | flops 25559040 | bytes 2359296 | tf_op jit(solution)/shard_map/convert_element_type | solution.py:100
  256.5 24.0 %reduce-scatter.9.cloned.1.call-done = bf16[4,192,128]{2,1,0:T(8,128)(2,1)} async-done(((bf16[4,768,128]{2,1,0:T(8,128)(2,1)}), bf16[4,192,128]{2,1,0:T(8,128)(2,1)}) %reduce-scatter.9.cloned.1.call-update) | async-done | bytes 196624 | tf_op jit(solution)/shard_map/reduce_scatter | solution.py:166
  280.5 2.9 fusion.33
  284.6 50.6 %all-gather.6.cloned.1.call-done = bf16[768,2560]{1,0:T(8,128)(2,1)} async-done(((bf16[192,2560]{1,0:T(8,128)(2,1)}), bf16[768,2560]{1,0:T(8,128)(2,1)}) %all-gather.6.cloned.1.call-update) | async-done | bytes 3932176 | tf_op jit(solution)/shard_map/all_gather | solution.py:184
  335.2 6.2 %fusion = f32[768,1024]{1,0:T(8,128)S(1)} fusion(bf16[2048,1024]{1,0:T(8,128)(2,1)} %param.14, bf16[768,2560]{1,0:T(8,128)(2,1)} %all-gather.6.cloned.1.call-done), kind=kOutput, calls=%fused_computation.1 | convolution fusion | flops 3221225472 | bytes 10485760 | tf_op jit(solution)/shard_map/dot_general | solution.py:190
  341.4 3.3 add_convert_fusion
  344.8 34.5 %reduce-scatter.11.cloned.1.call-done = bf16[96,1024]{1,0:T(8,128)(2,1)} async-done(((bf16[768,1024]{1,0:T(8,128)(2,1)}), bf16[96,1024]{1,0:T(8,128)(2,1)}) %reduce-scatter.11.cloned.1.call-update) | async-done | bytes 196624 | tf_op jit(solution)/shard_map/reduce_scatter | solution.py:187
  (71 shorter events, 16.2 us)
Async XLA Ops:
  6.5 47.8 %copy-start = (bf16[1024,1536]{1,0:T(8,128)(2,1)S(1)}, bf16[1024,1536]{1,0:T(8,128)(2,1)}, u32[]{:S(2)}) copy-start(bf16[1024,1536]{1,0:T(8,128)(2,1)} %param.11) | copy-start | bytes 9437188
  6.5 39.0 %all-gather.4.cloned.1.call-start = ((), (), s32[]{:S(2)}) async-start(), calls=%async_computation.4 | async-start | bytes 1769472 | tf_op jit(solution)/shard_map/all_gather | solution.py:80
  20.9 154.4 %reduce-scatter.7.cloned.1.call-start = ((), (), s32[]{:S(2)}) async-start(), calls=%async_computation.5 | async-start | bytes 13762560 | tf_op jit(solution)/shard_map/reduce_scatter | solution.py:91
  45.5 8.8 %copy-start.8 = (bf16[768,1024]{1,0:T(8,128)(2,1)S(1)}, bf16[768,1024]{1,0:T(8,128)(2,1)}, u32[]{:S(2)}) copy-start(bf16[768,1024]{1,0:T(8,128)(2,1)} %all-gather.4.cloned.1.call-done) | copy-start | bytes 4718596
  67.7 0.7 copy-start.9
  67.7 1.0 copy-start.7
  67.7 1.6 copy-start.10
  67.7 187.8 %reduce-scatter.13.cloned.1.call-start = ((), (), s32[]{:S(2)}) async-start(), calls=%async_computation.9 | async-start | bytes 245760
  183.9 23.0 %copy-start.6 = (bf16[224,512]{1,0:T(8,128)(2,1)S(1)}, bf16[224,512]{1,0:T(8,128)(2,1)}, u32[]{:S(2)}) copy-start(bf16[224,512]{1,0:T(8,128)(2,1)} %param.15) | copy-start | bytes 688132
  195.1 13.9 %copy-start.1 = (bf16[768,4,128]{2,0,1:T(8,128)(2,1)}, bf16[768,4,128]{2,0,1:T(8,128)(2,1)S(1)}, u32[]{:S(2)}) copy-start(bf16[768,4,128]{2,0,1:T(8,128)(2,1)S(1)} %all_gather.16) | copy-start | bytes 2359300
  227.4 53.1 %reduce-scatter.9.cloned.1.call-start = ((), (), s32[]{:S(2)}) async-start(), calls=%async_computation.6 | async-start | bytes 983040 | tf_op jit(solution)/shard_map/reduce_scatter | solution.py:166
  237.0 98.2 %all-gather.6.cloned.1.call-start = ((), (), s32[]{:S(2)}) async-start(), calls=%async_computation.7 | async-start | bytes 4915200 | tf_op jit(solution)/shard_map/all_gather | solution.py:184
  237.1 14.3 %copy-start.3 = (f32[192,3584]{1,0:T(8,128)S(1)}, f32[192,3584]{1,0:T(8,128)}, u32[]{:S(2)}) copy-start(f32[192,3584]{1,0:T(8,128)} %reduce-scatter.7.cloned.1.call-done) | copy-start | bytes 8257540
  280.5 3.0 copy-start.2
  284.5 94.7 %reduce-scatter.11.cloned.1.call-start = ((), (), s32[]{:S(2)}) async-start(), calls=%async_computation.8 | async-start | bytes 1769472 | tf_op jit(solution)/shard_map/reduce_scatter | solution.py:187
  335.2 6.2 %copy-start.5 = (bf16[512,1024]{1,0:T(8,128)(2,1)S(1)}, bf16[512,1024]{1,0:T(8,128)(2,1)}, u32[]{:S(2)}) copy-start(bf16[512,1024]{1,0:T(8,128)(2,1)} %param.13) | copy-start | bytes 3145732
  344.7 34.5 %copy-start.4 = (bf16[96,1024]{1,0:T(8,128)(2,1)S(1)}, bf16[96,1024]{1,0:T(8,128)(2,1)}, u32[]{:S(2)}) copy-start(bf16[96,1024]{1,0:T(8,128)(2,1)} %param.10) | copy-start | bytes 589828
Sparse Core Ops, SparseCore 0:
  21.1 24.4 all-gather.3
  67.9 107.4 reduce-scatter.6
  227.6 23.9 reduce-scatter.12
  254.4 26.1 reduce-scatter.8
  284.7 50.4 all-gather.5
  344.9 34.3 reduce-scatter.10
where the time goes:
time: 388 us
  waiting for transfers between devices  238 us (61%)
  blocking collectives  61.3 us (16%)
  matrix products  35.1 us (9%)
  other arithmetic  26.5 us (7%)
  between operations  13.7 us (4%)
  local copies, waits for them, and re-layouts  12.7 us (3%)
    reduce_scatter x1, waiting for transfers between devices, shards(): lax.psum_scatter(partial_sums, 'gx', scatter_dimension=0, tiled=True)  104 us
    all_gather x1, waiting for transfers between devices, shards(): gathered = lax.all_gather(joined, 'gx', axis=0, tiled=True)  50.6 us
    reduce_scatter x1, waiting for transfers between devices, shards(): lax.psum_scatter((jnp.dot(row_piece[:, :context_cols], out_weight, prefer...  34.5 us
    all_gather x1, waiting for transfers between devices, shards(): row_piece = lax.all_gather(normed, 'gy', axis=0, tiled=True)  24.5 us
    reduce_scatter x1, waiting for transfers between devices, shards(): lax.psum_scatter((cache_out * fading[..., None]).astype(jnp.bfloat16), 'g...  24 us
    pmax x1, blocking collectives, shards(): global_peak = lax.pmax(cache_peak, 'gx')  15.2 us
    all_gather x1, blocking collectives, shards(): lax.all_gather(own_values, 'gx', axis=0, tiled=True)  11.9 us
    all_gather x1, blocking collectives, shards(): lax.all_gather(own_keys, 'gx', axis=0, tiled=True)  11.6 us
  transfers between devices with their start and end apart: 6, of which 5 were waited for; matrix products, arithmetic and copies ran while one was open for 5% of the time, Pallas kernels for 0%

commit v1 on v0

--- a/solution.py
+++ b/solution.py
@@ -181,7 +181,12 @@
         jnp.transpose(context, (1, 0, 2)).reshape(share_rows, head_count * HD).astype(jnp.bfloat16)
     )
     joined = jnp.concatenate([context, hidden_own], axis=1)
-    gathered = lax.all_gather(joined, "gx", axis=0, tiled=True)
+    ring = [joined]
+    for hop in range(3):
+        ring.append(lax.ppermute(ring[-1], "gx", [(dev, (dev + 1) % 4) for dev in range(4)]))
+    gathered = jnp.roll(
+        jnp.concatenate(ring[::-1], axis=0), (lax.axis_index("gx") + 1) * ring[0].shape[0], axis=0
+    )
     context_cols = context.shape[1]
     row_piece = gathered
     mixed_sum = lax.psum_scatter(

time: 388 us -> 399 us (1.028)
  waiting for transfers between devices: 238 us -> 261 us
  matrix products: 35.1 us -> 25.8 us
  other arithmetic: 26.5 us -> 21.5 us
    ppermute x0 -> x3, waiting for transfers between devices: none -> 68.6 us  [shards(): lax.ppermute(ring[-1], 'gx', [(dev, (dev + 1) % 4) for dev in range(4)])]
    all_gather x1 -> x0, waiting for transfers between devices: 50.6 us -> none  [shards(): gathered = lax.all_gather(joined, 'gx', axis=0, tiled=True)]
    unnamed x25 -> x37, local copies, waits for them, and re-layouts: 2.36 us -> 7.35 us
  transfers between devices with their start and end apart: 6 -> 8, of which waited for: 5 -> 8; matrix products, arithmetic and copies ran while one was open for 5% -> 3% of each run, Pallas kernels for 0% -> 0%
where the time goes in v1:
time: 399 us; the launch traced here: 398 us
  waiting for transfers between devices  261 us (65%)
  blocking collectives  61.7 us (15%)
  matrix products  25.8 us (6%)
  other arithmetic  21.5 us (5%)
  between operations  13.5 us (3%)
  local copies, waits for them, and re-layouts  12.7 us (3%)
    reduce_scatter x1, waiting for transfers between devices, shards(): lax.psum_scatter(partial_sums, 'gx', scatter_dimension=0, tiled=True)  104 us
    ppermute x3, waiting for transfers between devices, shards(): lax.ppermute(ring[-1], 'gx', [(dev, (dev + 1) % 4) for dev in range(4)])  68.6 us
    reduce_scatter x1, waiting for transfers between devices, shards(): lax.psum_scatter((jnp.dot(row_piece[:, :context_cols], out_weight, prefer...  34.1 us
    reduce_scatter x1, waiting for transfers between devices, shards(): lax.psum_scatter((cache_out * fading[..., None]).astype(jnp.bfloat16), 'g...  27.9 us
    all_gather x1, waiting for transfers between devices, shards(): row_piece = lax.all_gather(normed, 'gy', axis=0, tiled=True)  24.5 us
    pmax x1, blocking collectives, shards(): global_peak = lax.pmax(cache_peak, 'gx')  15.4 us
    all_gather x1, blocking collectives, shards(): lax.all_gather(own_values, 'gx', axis=0, tiled=True)  12.3 us
    all_gather x1, blocking collectives, shards(): lax.all_gather(own_keys, 'gx', axis=0, tiled=True)  11.5 us
  transfers between devices with their start and end apart: 8, of which 8 were waited for; matrix products, arithmetic and copies ran while one was open for 3% of the time, Pallas kernels for 0%

profile of v1, /device:TPU:0, one launch (start us, length us, event | category | flops | bytes accessed | tf_op | source)
XLA Modules:
  0.0 398.4 jit_solution(7211729336010639907)
XLA Ops:
  7.8 11.4 %all-reduce = (f32[96]{0:T(128)S(1)}, f32[96]{0:T(128)S(1)}) all-reduce(f32[96]{0:T(128)S(1)} %get-tuple-element.20, f32[96]{0:T(128)S(1)} %get-tuple-element.19), channel_id=1, replica_groups=mesh['gx'=4,'gy'=8] {'gx'}, use_global_device_ids=true, to_apply=%region_7.8 | all-reduce | flops 192 | bytes 1536 | tf_op jit(solution)/shard_map/psum | solution.py:74
  19.1 1.8 fusion.40
  21.0 24.5 %all-gather.3.cloned.1.call-done = bf16[768,1024]{1,0:T(8,128)(2,1)} async-done(((bf16[96,1024]{1,0:T(8,128)(2,1)}), bf16[768,1024]{1,0:T(8,128)(2,1)}) %all-gather.3.cloned.1.call-update) | async-done | bytes 1572880 | tf_op jit(solution)/shard_map/all_gather | solution.py:80
  45.5 8.8 %fusion.62 = f32[768,2048]{1,0:T(8,128)} fusion(bf16[768,1024]{1,0:T(8,128)(2,1)} %all-gather.3.cloned.1.call-done, bf16[1024,2048]{1,0:T(8,128)(2,1)} %param.12), kind=kOutput, calls=%fused_computation.119 | convolution fusion | flops 3221225472 | bytes 12058624 | tf_op jit(solution)/shard_map/dot_general | solution.py:84
  54.3 4.3 %fusion.61 = f32[768,1536]{1,0:T(8,128)} fusion(bf16[768,1024]{1,0:T(8,128)(2,1)S(1)} %copy-done.10, bf16[1024,1536]{1,0:T(8,128)(2,1)S(1)} %copy-done), kind=kOutput, calls=%fused_computation.118 | convolution fusion | flops 2415919104 | bytes 9437184 | tf_op jit(solution)/shard_map/dot_general | solution.py:83
  58.6 9.1 %pad_maximum_fusion = f32[768,3584]{1,0:T(8,128)} fusion(f32[768,2048]{1,0:T(8,128)} %fusion.62, f32[768,1536]{1,0:T(8,128)} %fusion.61), kind=kLoop, calls=%fused_computation | loop fusion | flops 2752512 | bytes 22020096 | tf_op jit(solution)/shard_map/concatenate | solution.py:81
  70.9 104.4 %reduce-scatter.7.cloned.1.call-done = f32[192,3584]{1,0:T(8,128)} async-done(((f32[768,3584]{1,0:T(8,128)}), f32[192,3584]{1,0:T(8,128)}) %reduce-scatter.7.cloned.1.call-update) | async-done | bytes 2752528 | tf_op jit(solution)/shard_map/reduce_scatter | solution.py:91
  179.2 11.1 %all_gather.13 = bf16[768,4,128]{2,0,1:T(8,128)(2,1)S(1)} all-gather(bf16[192,4,128]{2,0,1:T(8,128)(2,1)S(1)} %pad_maximum_fusion.2), channel_id=1, replica_groups=mesh['gx'=4,'gy'=8] {'gx'}, dimensions={0}, use_global_device_ids=true | all-gather | bytes 983040 | tf_op jit(solution)/shard_map/all_gather | solution.py:96
  190.5 11.5 %all_gather.14 = bf16[768,4,128]{2,0,1:T(8,128)(2,1)} all-gather(bf16[192,4,128]{2,0,1:T(8,128)(2,1)S(1)} %pad_maximum_fusion.3), channel_id=1, replica_groups=mesh['gx'=4,'gy'=8] {'gx'}, dimensions={0}, use_global_device_ids=true | all-gather | bytes 983040 | tf_op jit(solution)/shard_map/all_gather | solution.py:97
  202.5 15.4 %pmax.7 = f32[4,768]{1,0:T(4,128)S(1)} all-reduce(f32[4,768]{1,0:T(4,128)S(1)} %broadcast_maximum_fusion), channel_id=1, replica_groups=mesh['gx'=4,'gy'=8] {'gx'}, use_global_device_ids=true, to_apply=%region_11.12 | all-reduce | flops 3072 | bytes 24576 | tf_op jit(solution)/shard_map/pmax | solution.py:160
  219.5 2.4 multiply_convert_fusion
  221.9 1.9 fusion.5
  223.9 1.8 slice.64
  225.8 12.3 %all-gather = bf16[768,4,1,128]{3,0,1,2:T(8,128)(2,1)} all-gather(bf16[192,4,1,128]{3,0,1,2:T(8,128)(2,1)S(1)} %copy.63), channel_id=2, replica_groups=mesh['gx'=4,'gy'=8] {'gx'}, dimensions={0}, use_global_device_ids=true | all-gather | bytes 983040 | tf_op jit(solution)/shard_map/all_gather | solution.py:98
  238.8 3.4 fusion.10
  244.7 27.9 %reduce-scatter.9.cloned.1.call-done = bf16[4,192,128]{2,1,0:T(8,128)(2,1)} async-done(((bf16[4,768,128]{2,1,0:T(8,128)(2,1)}), bf16[4,192,128]{2,1,0:T(8,128)(2,1)}) %reduce-scatter.9.cloned.1.call-update) | async-done | bytes 196624 | tf_op jit(solution)/shard_map/reduce_scatter | solution.py:166
  272.6 2.1 fusion.33
  276.2 22.9 %collective-permute-done = bf16[192,2560]{1,0:T(8,128)(2,1)S(1)} collective-permute-done((bf16[192,2560]{1,0:T(8,128)(2,1)S(1)}, bf16[192,2560]{1,0:T(8,128)(2,1)S(1)}, u32[]{:S(2)}, u32[]{:S(2)}) %collective-permute-start) | collective-permute-done | bytes 983072 | tf_op jit(solution)/shard_map/ppermute | solution.py:186
  299.7 22.9 %collective-permute-done.1 = bf16[192,2560]{1,0:T(8,128)(2,1)S(1)} collective-permute-done((bf16[192,2560]{1,0:T(8,128)(2,1)S(1)}, bf16[192,2560]{1,0:T(8,128)(2,1)S(1)}, u32[]{:S(2)}, u32[]{:S(2)}) %collective-permute-start.1) | collective-permute-done | bytes 983072 | tf_op jit(solution)/shard_map/ppermute | solution.py:186
  322.7 22.7 %collective-permute-done.2 = bf16[192,2560]{1,0:T(8,128)(2,1)} collective-permute-done((bf16[192,2560]{1,0:T(8,128)(2,1)S(1)}, bf16[192,2560]{1,0:T(8,128)(2,1)}, u32[]{:S(2)}, u32[]{:S(2)}) %collective-permute-start.2) | collective-permute-done | bytes 983072 | tf_op jit(solution)/shard_map/ppermute | solution.py:186
  348.3 2.0 copy-done.9
  350.3 3.6 fusion
  353.9 2.2 add_convert_fusion
  356.1 34.1 %reduce-scatter.11.cloned.1.call-done = bf16[96,1024]{1,0:T(8,128)(2,1)} async-done(((bf16[768,1024]{1,0:T(8,128)(2,1)}), bf16[96,1024]{1,0:T(8,128)(2,1)}) %reduce-scatter.11.cloned.1.call-update) | async-done | bytes 196624 | tf_op jit(solution)/shard_map/reduce_scatter | solution.py:192
  (89 shorter events, 20.5 us)
Async XLA Ops:
  6.5 47.8 %copy-start = (bf16[1024,1536]{1,0:T(8,128)(2,1)S(1)}, bf16[1024,1536]{1,0:T(8,128)(2,1)}, u32[]{:S(2)}) copy-start(bf16[1024,1536]{1,0:T(8,128)(2,1)} %param.11) | copy-start | bytes 9437188
  6.5 39.0 %all-gather.3.cloned.1.call-start = ((), (), s32[]{:S(2)}) async-start(), calls=%async_computation.4 | async-start | bytes 1769472 | tf_op jit(solution)/shard_map/all_gather | solution.py:80
  20.9 154.4 %reduce-scatter.7.cloned.1.call-start = ((), (), s32[]{:S(2)}) async-start(), calls=%async_computation.5 | async-start | bytes 13762560 | tf_op jit(solution)/shard_map/reduce_scatter | solution.py:91
  45.5 8.8 %copy-start.10 = (bf16[768,1024]{1,0:T(8,128)(2,1)S(1)}, bf16[768,1024]{1,0:T(8,128)(2,1)}, u32[]{:S(2)}) copy-start(bf16[768,1024]{1,0:T(8,128)(2,1)} %all-gather.3.cloned.1.call-done) | copy-start | bytes 4718596
  67.7 0.7 copy-start.12
  67.7 1.0 copy-start.8
  67.7 1.6 copy-start.13
  67.7 175.9 %reduce-scatter.13.cloned.1.call-start = ((), (), s32[]{:S(2)}) async-start(), calls=%async_computation.8 | async-start | bytes 245760
  175.3 1.3 slice-start
  177.5 1.2 copy-start.2
  179.0 23.0 %copy-start.7 = (bf16[224,512]{1,0:T(8,128)(2,1)S(1)}, bf16[224,512]{1,0:T(8,128)(2,1)}, u32[]{:S(2)}) copy-start(bf16[224,512]{1,0:T(8,128)(2,1)} %param.15) | copy-start | bytes 688132
  190.3 12.3 %copy-start.4 = (bf16[768,4,128]{2,0,1:T(8,128)(2,1)}, bf16[768,4,128]{2,0,1:T(8,128)(2,1)S(1)}, u32[]{:S(2)}) copy-start(bf16[768,4,128]{2,0,1:T(8,128)(2,1)S(1)} %all_gather.13) | copy-start | bytes 2359300
  202.5 17.0 %copy-start.11 = (bf16[224,512]{1,0:T(8,128)(2,1)S(1)}, bf16[224,512]{1,0:T(8,128)(2,1)}, u32[]{:S(2)}) copy-start(bf16[224,512]{1,0:T(8,128)(2,1)} %param.16) | copy-start | bytes 688132
  219.5 53.1 %reduce-scatter.9.cloned.1.call-start = ((), (), s32[]{:S(2)}) async-start(), calls=%async_computation.6 | async-start | bytes 983040 | tf_op jit(solution)/shard_map/reduce_scatter | solution.py:166
  225.8 164.4 %reduce-scatter.11.cloned.1.call-start = ((), (), s32[]{:S(2)}) async-start(), calls=%async_computation.7 | async-start | bytes 1769472 | tf_op jit(solution)/shard_map/reduce_scatter | solution.py:192
  225.8 13.0 %copy-start.3 = (f32[192,3584]{1,0:T(8,128)S(1)}, f32[192,3584]{1,0:T(8,128)}, u32[]{:S(2)}) copy-start(f32[192,3584]{1,0:T(8,128)} %reduce-scatter.7.cloned.1.call-done) | copy-start | bytes 8257540
  274.8 24.4 %collective-permute-start = (bf16[192,2560]{1,0:T(8,128)(2,1)S(1)}, bf16[192,2560]{1,0:T(8,128)(2,1)S(1)}, u32[]{:S(2)}, u32[]{:S(2)}) collective-permute-start(bf16[192,2560]{1,0:T(8,128)(2,1)S(1)} %pad_maximum_fusion.1), channel_id=1, source_target_pairs={{0,8},{8,16},{16,24},{24,0},{1,9},{9,17},{17,25},{25,1},{2,10},{10... | collective-permute-start | bytes 2949128 | tf_op jit(solution)/shard_map/ppermute | solution.py:186
  299.2 23.5 %collective-permute-start.1 = (bf16[192,2560]{1,0:T(8,128)(2,1)S(1)}, bf16[192,2560]{1,0:T(8,128)(2,1)S(1)}, u32[]{:S(2)}, u32[]{:S(2)}) collective-permute-start(bf16[192,2560]{1,0:T(8,128)(2,1)S(1)} %collective-permute-done), channel_id=1, source_target_pairs={{0,8},{8,16},{16,24},{24,0},{1,9},{9,17},{17,25},{25,1},{2,10},{10... | collective-permute-start | bytes 2949128 | tf_op jit(solution)/shard_map/ppermute | solution.py:186
  322.7 22.7 %collective-permute-start.2 = (bf16[192,2560]{1,0:T(8,128)(2,1)S(1)}, bf16[192,2560]{1,0:T(8,128)(2,1)}, u32[]{:S(2)}, u32[]{:S(2)}) collective-permute-start(bf16[192,2560]{1,0:T(8,128)(2,1)S(1)} %collective-permute-done.1), channel_id=1, source_target_pairs={{0,8},{8,16},{16,24},{24,0},{1,9},{9,17},{17,25},{25,1},{2,10},{10... | collective-permute-start | bytes 2949128 | tf_op jit(solution)/shard_map/ppermute | solution.py:186
  348.1 2.2 copy-start.9
  350.3 3.6 copy-start.6
  353.9 36.3 %copy-start.5 = (bf16[96,1024]{1,0:T(8,128)(2,1)S(1)}, bf16[96,1024]{1,0:T(8,128)(2,1)}, u32[]{:S(2)}) copy-start(bf16[96,1024]{1,0:T(8,128)(2,1)} %param.10) | copy-start | bytes 589828
  353.9 38.0 %copy-start.1 = (bf16[1024,1536]{1,0:T(8,128)(2,1)S(1)}, bf16[1024,1536]{1,0:T(8,128)(2,1)}, u32[]{:S(2)}) copy-start(bf16[1024,1536]{1,0:T(8,128)(2,1)} %param.11) | copy-start | bytes 9437188
Sparse Core Ops, SparseCore 0:
  21.1 24.4 all-gather.2
  67.9 107.4 reduce-scatter.6
  219.6 24.0 reduce-scatter.12
  246.4 26.0 reduce-scatter.8
  356.2 33.9 reduce-scatter.10
